TPU v7x, 512 devices: a whole 4x8x8 slice. The times are simulated.
512 devices in a mesh: band: 32 (over z_lo, y, core), dom: 16 (over z_hi, x).
Axes of the slice: x: 4, y: 8, z: 8 (z_hi: 4, z_lo: 2; z = z_hi * 2 + z_lo), core: 2. Of those that a mesh axis runs over, the one named last changes fastest.
Arguments:
- states: float32 [4096, 8, 128, 128], P('band', None, 'dom'), may hold values from -0.015625 to 0.015625
- window: float32 [128, 8, 128, 128], P('band', None, 'dom'), may hold values from -6 to 6
- potential: float32 [8, 128, 128], P(None, 'dom'), may hold values from -3 to 3
Outputs:
- intersection: float32 [4096, 128], P('band')
- hamiltonian: float32 [4096, 128], P('band')
All inputs are finite; a program needn't handle non-finite values.
Results may differ from a plain program's by a relative error of at most 0.00012.
Values sent between devices are 32-bit elements; how exact they have to be, the bound alone decides.
A program may use at most 64 MiB of HBM per device.

v0:
```python
import jax
import jax.numpy as jnp
from jax import lax
from jax.sharding import PartitionSpec as P

DEGREE = 4
coeffs = (
    -5369.0 / 1800.0,
    12.0 / 7.0,
    -15.0 / 56.0,
    10.0 / 189.0,
    -1.0 / 112.0,
    2.0 / 1925.0,
    -1.0 / 16632.0,
)
centre_value = 9.0
half_width = 7.0


def padded(block, sides, width):
    for axis, dim in sides:
        count = lax.axis_size(axis)
        forward = [(i, i + 1) for i in range(count - 1)]
        forward.append((count - 1, 0))
        backward = [(target, source) for source, target in forward]
        low = lax.ppermute(
            lax.slice_in_dim(block, block.shape[dim] - width, None, axis=dim), axis, forward
        )
        high = lax.ppermute(lax.slice_in_dim(block, 0, width, axis=dim), axis, backward)
        block = jnp.concatenate([low, block, high], axis=dim)
    return block


def stencil_sum(wave_in, padded_x, padded_y, potential):
    x_cells = wave_in.shape[2]
    y_cells = wave_in.shape[3]
    z_cells = wave_in.shape[1]
    along_z = jnp.pad(wave_in, ((0, 0), (6, 6), (0, 0), (0, 0)))
    laplace = 3.0 * coeffs[0] * wave_in
    for offset in range(1, 7):
        beside = (
            padded_x[:, :, 6 + offset : 6 + offset + x_cells]
            + padded_x[:, :, 6 - offset : 6 - offset + x_cells]
        )
        beside = (
            beside
            + padded_y[:, :, :, 6 + offset : 6 + offset + y_cells]
            + padded_y[:, :, :, 6 - offset : 6 - offset + y_cells]
        )
        beside = (
            beside
            + along_z[:, 6 + offset : 6 + offset + z_cells]
            + along_z[:, 6 - offset : 6 - offset + z_cells]
        )
        laplace = laplace + coeffs[offset] * beside
    return -0.5 * laplace + potential * wave_in


def apply_banded(wave_in, potential):
    padded_x = padded(wave_in, (("dom", 2),), 6)
    padded_y = jnp.concatenate((wave_in[:, :, :, -6:], wave_in, wave_in[:, :, :, :6]), axis=3)
    return stencil_sum(wave_in, padded_x, padded_y, potential)


def chebyshev(window, operate):
    previous = window
    current = (operate(window) - centre_value * window) / half_width
    for repeat_index in range(DEGREE - 1):
        following = 2.0 * (operate(current) - centre_value * current) / half_width - previous
        previous, current = (current, following)
    image = operate(current)
    return jnp.stack((current, image))


def per_device(states, window, potential):
    stacked = chebyshev(window, lambda wave: apply_banded(wave, potential))
    states_flat = states.reshape(states.shape[0], -1)
    whole_window = lax.all_gather(stacked, "band", axis=1, tiled=True)
    flat_piece = whole_window.reshape(-1, states_flat.shape[1])
    product = lax.dot_general(
        states_flat,
        flat_piece,
        (((1,), (1,)), ((), ())),
        precision=lax.Precision.HIGHEST,
        preferred_element_type=jnp.float32,
    )
    partial_value = product.reshape(states_flat.shape[0], 2, whole_window.shape[1])
    totals = lax.psum(partial_value, "dom")
    return (totals[:, 0, :], totals[:, 1, :])


def solution(mesh):
    in_specs = (P("band", None, "dom", None), P("band", None, "dom", None), P(None, "dom", None))
    out_specs = (P("band", None), P("band", None))
    return jax.shard_map(
        per_device, mesh=mesh, in_specs=in_specs, out_specs=out_specs, check_vma=False
    )
```

profile of v0, /device:TPU:8, one launch (start us, length us, event | category | flops | bytes accessed | tf_op | source)
XLA Modules:
  0.0 371.7 jit_solution(3588212571015930287)
XLA Ops:
  7.2 0.0 copy-start
  7.2 0.0 all-gather.2.cloned.1.call-start
  7.2 1.0 fusion.338
  8.2 13.1 %collective-permute-start = (f32[4,8,6,128]{3,2,1,0:T(8,128)S(1)}, f32[4,8,6,128]{3,2,1,0:T(8,128)S(1)}, u32[]{:S(2)}, u32[]{:S(2)}) collective-permute-start(f32[4,8,6,128]{3,2,1,0:T(8,128)S(1)} %get-tuple-element.22), channel_id=1, source_target_pairs={{1,0},{2,1},{3,2},{4,3},{5,4},{6,5},{7,6},{8,7},{9,8},{10,9},{11,1... | collective-permute-start | bytes 294920 | tf_op jit(solution)/shard_map/ppermute | solution.py:29
  21.4 1.9 collective-permute-start.1
  23.3 1.1 fusion.339
  24.4 0.8 broadcast_multiply_fusion.1
  25.1 0.9 constant_dynamic-update-slice_fusion.1
  26.1 0.8 collective-permute-done
  26.9 7.5 %collective-permute-done.1 = f32[4,8,6,128]{3,2,1,0:T(8,128)S(1)} collective-permute-done((f32[4,8,6,128]{3,2,1,0:T(8,128)S(1)}, f32[4,8,6,128]{3,2,1,0:T(8,128)S(1)}, u32[]{:S(2)}, u32[]{:S(2)}) %collective-permute-start.1) | collective-permute-done | bytes 98336 | tf_op jit(solution)/shard_map/ppermute | solution.py:26
  34.5 5.2 %broadcast_multiply_fusion = (f32[4,8,8,128]{3,2,1,0:T(8,128)S(1)}, f32[4,8,8,128]{3,2,1,0:T(8,128)S(1)}) fusion(f32[4,8,8,128]{3,2,1,0:T(8,128)} %param.4, f32[8,8,128]{2,1,0:T(8,128)} %param.5, f32[4,8,8,6]{3,2,1,0:T(8,128)S(1)} %get-tuple-element.25, f32[4,8,8,6]{3,2,1,0:T(8,128)S(1)} %get-tuple-element.24, ...), kind=kLoop, calls=%fused_computation.601 | loop fusion | flops 2195456 | bytes 1323008 | tf_op jit(solution)/shard_map/div | solution.py:67
  39.7 1.9 collective-permute-start.2
  41.6 3.9 %collective-permute-start.3 = (f32[4,8,6,128]{3,2,1,0:T(8,128)S(1)}, f32[4,8,6,128]{3,2,1,0:T(8,128)S(1)}, u32[]{:S(2)}, u32[]{:S(2)}) collective-permute-start(f32[4,8,6,128]{3,2,1,0:T(8,128)S(1)} %get-tuple-element.19), channel_id=1, source_target_pairs={{0,1},{1,2},{2,3},{3,4},{4,5},{5,6},{6,7},{7,8},{8,9},{9,10},{10,1... | collective-permute-start | bytes 294920 | tf_op jit(solution)/shard_map/ppermute | solution.py:26
  45.6 0.1 fusion.337
  45.7 1.8 collective-permute-done.2
  47.5 7.0 %collective-permute-done.3 = f32[4,8,6,128]{3,2,1,0:T(8,128)S(1)} collective-permute-done((f32[4,8,6,128]{3,2,1,0:T(8,128)S(1)}, f32[4,8,6,128]{3,2,1,0:T(8,128)S(1)}, u32[]{:S(2)}, u32[]{:S(2)}) %collective-permute-start.3) | collective-permute-done | bytes 98336 | tf_op jit(solution)/shard_map/ppermute | solution.py:26
  54.5 1.8 fusion.195
  56.2 1.9 collective-permute-start.4
  58.2 3.9 %collective-permute-start.5 = (f32[4,8,6,128]{3,2,1,0:T(8,128)S(1)}, f32[4,8,6,128]{3,2,1,0:T(8,128)S(1)}, u32[]{:S(2)}, u32[]{:S(2)}) collective-permute-start(f32[4,8,6,128]{3,2,1,0:T(8,128)S(1)} %get-tuple-element.15), channel_id=1, source_target_pairs={{0,1},{1,2},{2,3},{3,4},{4,5},{5,6},{6,7},{7,8},{8,9},{9,10},{10,1... | collective-permute-start | bytes 294920 | tf_op jit(solution)/shard_map/ppermute | solution.py:26
  62.1 0.1 fusion.335
  62.2 0.9 collective-permute-done.4
  63.1 6.2 %collective-permute-done.5 = f32[4,8,6,128]{3,2,1,0:T(8,128)S(1)} collective-permute-done((f32[4,8,6,128]{3,2,1,0:T(8,128)S(1)}, f32[4,8,6,128]{3,2,1,0:T(8,128)S(1)}, u32[]{:S(2)}, u32[]{:S(2)}) %collective-permute-start.5) | collective-permute-done | bytes 98336 | tf_op jit(solution)/shard_map/ppermute | solution.py:26
  69.3 1.6 fusion.134
  70.9 1.9 collective-permute-start.6
  72.9 3.9 %collective-permute-start.7 = (f32[4,8,6,128]{3,2,1,0:T(8,128)S(1)}, f32[4,8,6,128]{3,2,1,0:T(8,128)S(1)}, u32[]{:S(2)}, u32[]{:S(2)}) collective-permute-start(f32[4,8,6,128]{3,2,1,0:T(8,128)S(1)} %get-tuple-element.11), channel_id=1, source_target_pairs={{0,1},{1,2},{2,3},{3,4},{4,5},{5,6},{6,7},{7,8},{8,9},{9,10},{10,1... | collective-permute-start | bytes 294920 | tf_op jit(solution)/shard_map/ppermute | solution.py:26
  76.8 0.1 fusion.333
  76.9 0.9 collective-permute-done.6
  77.8 6.8 %collective-permute-done.7 = f32[4,8,6,128]{3,2,1,0:T(8,128)S(1)} collective-permute-done((f32[4,8,6,128]{3,2,1,0:T(8,128)S(1)}, f32[4,8,6,128]{3,2,1,0:T(8,128)S(1)}, u32[]{:S(2)}, u32[]{:S(2)}) %collective-permute-start.7) | collective-permute-done | bytes 98336 | tf_op jit(solution)/shard_map/ppermute | solution.py:26
  84.6 0.0 copy-done
  84.6 0.9 fusion.73
  85.5 1.9 collective-permute-start.8
  87.4 3.9 %collective-permute-start.9 = (f32[4,8,6,128]{3,2,1,0:T(8,128)S(1)}, f32[4,8,6,128]{3,2,1,0:T(8,128)S(1)}, u32[]{:S(2)}, u32[]{:S(2)}) collective-permute-start(f32[4,8,6,128]{3,2,1,0:T(8,128)S(1)} %get-tuple-element.7), channel_id=1, source_target_pairs={{0,1},{1,2},{2,3},{3,4},{4,5},{5,6},{6,7},{7,8},{8,9},{9,10},{10,1... | collective-permute-start | bytes 294920 | tf_op jit(solution)/shard_map/ppermute | solution.py:26
  91.3 0.1 fusion.331
  91.4 0.9 collective-permute-done.8
  92.3 6.1 %collective-permute-done.9 = f32[4,8,6,128]{3,2,1,0:T(8,128)S(1)} collective-permute-done((f32[4,8,6,128]{3,2,1,0:T(8,128)S(1)}, f32[4,8,6,128]{3,2,1,0:T(8,128)S(1)}, u32[]{:S(2)}, u32[]{:S(2)}) %collective-permute-start.9) | collective-permute-done | bytes 98336 | tf_op jit(solution)/shard_map/ppermute | solution.py:26
  98.5 0.9 fusion.12
  99.3 0.7 pad_maximum_fusion
  100.1 0.0 all-gather.2.cloned.1.call-update
  100.1 0.0 all-reduce.7.cloned.1.call-start
  100.1 69.7 %all-gather.2.cloned.1.call-done = f32[2,128,8,8,128]{4,3,2,1,0:T(8,128)} async-done(((f32[2,4,8,8,128]{4,3,2,1,0:T(8,128)}), f32[2,128,8,8,128]{4,3,2,1,0:T(8,128)}) %all-gather.2.cloned.1.call-update) | async-done | bytes 8388624 | tf_op jit(solution)/shard_map/all_gather | solution.py:78
  169.9 9.4 %reshape.14 = f32[256,8192]{1,0:T(8,128)} reshape(f32[2,128,8,8,128]{4,3,2,1,0:T(8,128)} %all-gather.2.cloned.1.call-done) | data formatting | bytes 16777216 | tf_op jit(solution)/shard_map/reshape | solution.py:79
  179.2 11.7 %fusion = f32[256,128]{1,0:T(8,128)S(1)} fusion(f32[256,8192]{1,0:T(8,128)} %reshape.14, f32[16,8,64,128]{3,2,1,0:T(8,128)} %bitcast.19), kind=kOutput, calls=%fused_computation | convolution fusion | flops 3221225472 | bytes 12713984 | tf_op jit(solution)/shard_map/dot_general | solution.py:80
  191.0 0.7 copy.5
  191.7 0.0 all-reduce.7.cloned.1.call-update
  191.7 171.6 %all-reduce.7.cloned.1.call-done = f32[128,2,128]{2,0,1:T(8,128)} async-done(((f32[128,2,128]{2,0,1:T(8,128)}), f32[128,2,128]{2,0,1:T(8,128)}) %all-reduce.7.cloned.1.call-update) | async-done | bytes 131088 | tf_op jit(solution)/shard_map/psum | solution.py:88
  363.4 1.5 slice_bitcast_fusion
  (5 shorter events, 0.1 us)
Async XLA Ops:
  7.2 77.4 %copy-start = (f32[8,8,128]{2,1,0:T(8,128)S(1)}, f32[8,8,128]{2,1,0:T(8,128)}, u32[]{:S(2)}) copy-start(f32[8,8,128]{2,1,0:T(8,128)} %param.5) | copy-start | bytes 98308
  7.2 162.7 %all-gather.2.cloned.1.call-start = ((), (), s32[]{:S(2)}) async-start(), calls=%async_computation | async-start | bytes 8650752 | tf_op jit(solution)/shard_map/all_gather | solution.py:78
  8.2 18.7 %collective-permute-start = (f32[4,8,6,128]{3,2,1,0:T(8,128)S(1)}, f32[4,8,6,128]{3,2,1,0:T(8,128)S(1)}, u32[]{:S(2)}, u32[]{:S(2)}) collective-permute-start(f32[4,8,6,128]{3,2,1,0:T(8,128)S(1)} %get-tuple-element.22), channel_id=1, source_target_pairs={{1,0},{2,1},{3,2},{4,3},{5,4},{6,5},{7,6},{8,7},{9,8},{10,9},{11,1... | collective-permute-start | bytes 294920 | tf_op jit(solution)/shard_map/ppermute | solution.py:29
  21.4 13.1 %collective-permute-start.1 = (f32[4,8,6,128]{3,2,1,0:T(8,128)S(1)}, f32[4,8,6,128]{3,2,1,0:T(8,128)S(1)}, u32[]{:S(2)}, u32[]{:S(2)}) collective-permute-start(f32[4,8,6,128]{3,2,1,0:T(8,128)S(1)} %get-tuple-element.23), channel_id=1, source_target_pairs={{0,1},{1,2},{2,3},{3,4},{4,5},{5,6},{6,7},{7,8},{8,9},{9,10},{10,1... | collective-permute-start | bytes 294920 | tf_op jit(solution)/shard_map/ppermute | solution.py:26
  39.7 7.8 %collective-permute-start.2 = (f32[4,8,6,128]{3,2,1,0:T(8,128)S(1)}, f32[4,8,6,128]{3,2,1,0:T(8,128)S(1)}, u32[]{:S(2)}, u32[]{:S(2)}) collective-permute-start(f32[4,8,6,128]{3,2,1,0:T(8,128)S(1)} %get-tuple-element.18), channel_id=1, source_target_pairs={{1,0},{2,1},{3,2},{4,3},{5,4},{6,5},{7,6},{8,7},{9,8},{10,9},{11,1... | collective-permute-start | bytes 294920 | tf_op jit(solution)/shard_map/ppermute | solution.py:29
  41.6 12.8 %collective-permute-start.3 = (f32[4,8,6,128]{3,2,1,0:T(8,128)S(1)}, f32[4,8,6,128]{3,2,1,0:T(8,128)S(1)}, u32[]{:S(2)}, u32[]{:S(2)}) collective-permute-start(f32[4,8,6,128]{3,2,1,0:T(8,128)S(1)} %get-tuple-element.19), channel_id=1, source_target_pairs={{0,1},{1,2},{2,3},{3,4},{4,5},{5,6},{6,7},{7,8},{8,9},{9,10},{10,1... | collective-permute-start | bytes 294920 | tf_op jit(solution)/shard_map/ppermute | solution.py:26
  56.2 6.9 %collective-permute-start.4 = (f32[4,8,6,128]{3,2,1,0:T(8,128)S(1)}, f32[4,8,6,128]{3,2,1,0:T(8,128)S(1)}, u32[]{:S(2)}, u32[]{:S(2)}) collective-permute-start(f32[4,8,6,128]{3,2,1,0:T(8,128)S(1)} %get-tuple-element.14), channel_id=1, source_target_pairs={{1,0},{2,1},{3,2},{4,3},{5,4},{6,5},{7,6},{8,7},{9,8},{10,9},{11,1... | collective-permute-start | bytes 294920 | tf_op jit(solution)/shard_map/ppermute | solution.py:29
  58.2 11.1 %collective-permute-start.5 = (f32[4,8,6,128]{3,2,1,0:T(8,128)S(1)}, f32[4,8,6,128]{3,2,1,0:T(8,128)S(1)}, u32[]{:S(2)}, u32[]{:S(2)}) collective-permute-start(f32[4,8,6,128]{3,2,1,0:T(8,128)S(1)} %get-tuple-element.15), channel_id=1, source_target_pairs={{0,1},{1,2},{2,3},{3,4},{4,5},{5,6},{6,7},{7,8},{8,9},{9,10},{10,1... | collective-permute-start | bytes 294920 | tf_op jit(solution)/shard_map/ppermute | solution.py:26
  70.9 6.9 %collective-permute-start.6 = (f32[4,8,6,128]{3,2,1,0:T(8,128)S(1)}, f32[4,8,6,128]{3,2,1,0:T(8,128)S(1)}, u32[]{:S(2)}, u32[]{:S(2)}) collective-permute-start(f32[4,8,6,128]{3,2,1,0:T(8,128)S(1)} %get-tuple-element.10), channel_id=1, source_target_pairs={{1,0},{2,1},{3,2},{4,3},{5,4},{6,5},{7,6},{8,7},{9,8},{10,9},{11,1... | collective-permute-start | bytes 294920 | tf_op jit(solution)/shard_map/ppermute | solution.py:29
  72.9 11.7 %collective-permute-start.7 = (f32[4,8,6,128]{3,2,1,0:T(8,128)S(1)}, f32[4,8,6,128]{3,2,1,0:T(8,128)S(1)}, u32[]{:S(2)}, u32[]{:S(2)}) collective-permute-start(f32[4,8,6,128]{3,2,1,0:T(8,128)S(1)} %get-tuple-element.11), channel_id=1, source_target_pairs={{0,1},{1,2},{2,3},{3,4},{4,5},{5,6},{6,7},{7,8},{8,9},{9,10},{10,1... | collective-permute-start | bytes 294920 | tf_op jit(solution)/shard_map/ppermute | solution.py:26
  85.5 6.9 %collective-permute-start.8 = (f32[4,8,6,128]{3,2,1,0:T(8,128)S(1)}, f32[4,8,6,128]{3,2,1,0:T(8,128)S(1)}, u32[]{:S(2)}, u32[]{:S(2)}) collective-permute-start(f32[4,8,6,128]{3,2,1,0:T(8,128)S(1)} %get-tuple-element.6), channel_id=1, source_target_pairs={{1,0},{2,1},{3,2},{4,3},{5,4},{6,5},{7,6},{8,7},{9,8},{10,9},{11,1... | collective-permute-start | bytes 294920 | tf_op jit(solution)/shard_map/ppermute | solution.py:29
  87.4 11.1 %collective-permute-start.9 = (f32[4,8,6,128]{3,2,1,0:T(8,128)S(1)}, f32[4,8,6,128]{3,2,1,0:T(8,128)S(1)}, u32[]{:S(2)}, u32[]{:S(2)}) collective-permute-start(f32[4,8,6,128]{3,2,1,0:T(8,128)S(1)} %get-tuple-element.7), channel_id=1, source_target_pairs={{0,1},{1,2},{2,3},{3,4},{4,5},{5,6},{6,7},{7,8},{8,9},{9,10},{10,1... | collective-permute-start | bytes 294920 | tf_op jit(solution)/shard_map/ppermute | solution.py:26
  100.1 263.3 %all-reduce.7.cloned.1.call-start = ((), (), s32[]{:S(2)}) async-start(), calls=%async_computation.1 | async-start | bytes 262144 | tf_op jit(solution)/shard_map/psum | solution.py:88
Sparse Core Ops, SparseCore 0:
  100.2 69.6 all-gather.1
  191.9 171.4 all-reduce.6
where the time goes:
time: 373 us; the launch traced here: 372 us
  waiting for transfers between devices  280 us (75%)
  starting transfers between devices  38.5 us (10%)
  local copies, waits for them, and re-layouts  15.1 us (4%)
  between operations  14.2 us (4%)
  other arithmetic  11.8 us (3%)
  matrix products  11.7 us (3%)
    psum x1, waiting for transfers between devices, per_device(): totals = lax.psum(partial_value, 'dom')  172 us
    all_gather x1, waiting for transfers between devices, per_device(): whole_window = lax.all_gather(stacked, 'band', axis=1, tiled=True)  69.7 us
    ppermute x5, waiting for transfers between devices, padded(): lax.ppermute(lax.slice_in_dim(block, block.shape[dim] - width, None, axis...  33.6 us
    ppermute x5, starting transfers between devices, padded(): lax.ppermute(lax.slice_in_dim(block, 0, width, axis=dim), axis, backward)  20.8 us
    ppermute x5, starting transfers between devices, padded(): lax.ppermute(lax.slice_in_dim(block, block.shape[dim] - width, None, axis...  17.6 us
    dot_general x1, matrix products, per_device(): lax.dot_general(states_flat, flat_piece, (((1,), (1,)), ((), ())), precis...  11.7 us
    reshape x1, local copies, waits for them, and re-layouts, per_device(): flat_piece = whole_window.reshape(-1, states_flat.shape[1])  9.36 us
  transfers between devices with their start and end apart: 12, of which 12 were waited for; matrix products, arithmetic and copies ran while one was open for 1% of the time, Pallas kernels for 0%

commit v1 on v0

--- a/solution.py
+++ b/solution.py
@@ -75,7 +75,9 @@
 def per_device(states, window, potential):
     stacked = chebyshev(window, lambda wave: apply_banded(wave, potential))
     states_flat = states.reshape(states.shape[0], -1)
-    whole_window = lax.all_gather(stacked, "band", axis=1, tiled=True)
+    whole_window = jnp.concatenate(
+        lax.all_to_all(jnp.stack(lax.psum(1, "band") * [stacked], axis=0), "band", 0, 0), axis=1
+    )
     flat_piece = whole_window.reshape(-1, states_flat.shape[1])
     product = lax.dot_general(
         states_flat,

time: 373 us -> 493 us (1.32)
  blocking collectives: 0 us -> 196 us
  waiting for transfers between devices: 280 us -> 200 us
  local copies, waits for them, and re-layouts: 15.1 us -> 20.2 us
    all_to_all x0 -> x1, blocking collectives: none -> 196 us  [per_device(): lax.all_to_all(jnp.stack(lax.psum(1, 'band') * [stacked], axis=0), 'band'...]
    all_gather x1 -> x0, waiting for transfers between devices: 69.7 us -> none  [per_device(): whole_window = lax.all_gather(stacked, 'band', axis=1, tiled=True)]
    another operation x0 -> x2, local copies, waits for them, and re-layouts: none -> 10.4 us  [the longest x1 9.37 us: per_device(): flat_piece = whole_window.reshape(-1, states_flat.shape[1])]
    psum x1, waiting for transfers between devices: 172 us -> 161 us  [per_device(): totals = lax.psum(partial_value, 'dom')]
    reshape x1, local copies, waits for them, and re-layouts: 9.36 us -> 4.1 us  [per_device(): jnp.concatenate(lax.all_to_all(jnp.stack(lax.psum(1, 'band') * [stacked],...]
  transfers between devices with their start and end apart: 12 -> 11, of which waited for: 12 -> 11; matrix products, arithmetic and copies ran while one was open for 1% -> 1% of each run, Pallas kernels for 0% -> 0%
where the time goes in v1:
time: 493 us; the launch traced here: 492 us
  waiting for transfers between devices  200 us (41%)
  blocking collectives  196 us (40%)
  starting transfers between devices  38.5 us (8%)
  local copies, waits for them, and re-layouts  20.2 us (4%)
  between operations  14.2 us (3%)
  matrix products  11.7 us (2%)
  other arithmetic  11.1 us (2%)
    all_to_all x1, blocking collectives, per_device(): lax.all_to_all(jnp.stack(lax.psum(1, 'band') * [stacked], axis=0), 'band'...  196 us
    psum x1, waiting for transfers between devices, per_device(): totals = lax.psum(partial_value, 'dom')  161 us
    ppermute x5, waiting for transfers between devices, padded(): lax.ppermute(lax.slice_in_dim(block, block.shape[dim] - width, None, axis...  33.6 us
    ppermute x5, starting transfers between devices, padded(): lax.ppermute(lax.slice_in_dim(block, 0, width, axis=dim), axis, backward)  20.8 us
    ppermute x5, starting transfers between devices, padded(): lax.ppermute(lax.slice_in_dim(block, block.shape[dim] - width, None, axis...  17.6 us
    dot_general x1, matrix products, per_device(): lax.dot_general(states_flat, flat_piece, (((1,), (1,)), ((), ())), precis...  11.7 us
  transfers between devices with their start and end apart: 11, of which 11 were waited for; matrix products, arithmetic and copies ran while one was open for 1% of the time, Pallas kernels for 0%

profile of v1, /device:TPU:8, one launch (start us, length us, event | category | flops | bytes accessed | tf_op | source)
XLA Modules:
  0.0 492.2 jit_solution(3551801408100975676)
XLA Ops:
  7.2 0.0 copy-start
  7.2 0.0 all-reduce.7.cloned.1.call-start
  7.2 1.0 fusion.338
  8.2 13.1 %collective-permute-start = (f32[4,8,6,128]{3,2,1,0:T(8,128)S(1)}, f32[4,8,6,128]{3,2,1,0:T(8,128)S(1)}, u32[]{:S(2)}, u32[]{:S(2)}) collective-permute-start(f32[4,8,6,128]{3,2,1,0:T(8,128)S(1)} %get-tuple-element.22), channel_id=1, source_target_pairs={{1,0},{2,1},{3,2},{4,3},{5,4},{6,5},{7,6},{8,7},{9,8},{10,9},{11,1... | collective-permute-start | bytes 294920 | tf_op jit(solution)/shard_map/ppermute | solution.py:29
  21.4 1.9 collective-permute-start.1
  23.3 1.1 fusion.339
  24.4 0.8 broadcast_multiply_fusion.1
  25.1 0.9 constant_dynamic-update-slice_fusion.1
  26.1 0.8 collective-permute-done
  26.9 7.5 %collective-permute-done.1 = f32[4,8,6,128]{3,2,1,0:T(8,128)S(1)} collective-permute-done((f32[4,8,6,128]{3,2,1,0:T(8,128)S(1)}, f32[4,8,6,128]{3,2,1,0:T(8,128)S(1)}, u32[]{:S(2)}, u32[]{:S(2)}) %collective-permute-start.1) | collective-permute-done | bytes 98336 | tf_op jit(solution)/shard_map/ppermute | solution.py:26
  34.5 5.2 %broadcast_multiply_fusion = (f32[4,8,8,128]{3,2,1,0:T(8,128)S(1)}, f32[4,8,8,128]{3,2,1,0:T(8,128)S(1)}) fusion(f32[4,8,8,128]{3,2,1,0:T(8,128)} %param.4, f32[8,8,128]{2,1,0:T(8,128)} %param.5, f32[4,8,8,6]{3,2,1,0:T(8,128)S(1)} %get-tuple-element.25, f32[4,8,8,6]{3,2,1,0:T(8,128)S(1)} %get-tuple-element.24, ...), kind=kLoop, calls=%fused_computation.601 | loop fusion | flops 2195456 | bytes 1323008 | tf_op jit(solution)/shard_map/div | solution.py:67
  39.7 1.9 collective-permute-start.2
  41.6 3.9 collective-permute-start.3
  45.6 0.1 fusion.337
  45.7 1.8 collective-permute-done.2
  47.5 7.0 %collective-permute-done.3 = f32[4,8,6,128]{3,2,1,0:T(8,128)S(1)} collective-permute-done((f32[4,8,6,128]{3,2,1,0:T(8,128)S(1)}, f32[4,8,6,128]{3,2,1,0:T(8,128)S(1)}, u32[]{:S(2)}, u32[]{:S(2)}) %collective-permute-start.3) | collective-permute-done | bytes 98336 | tf_op jit(solution)/shard_map/ppermute | solution.py:26
  54.5 1.8 fusion.195
  56.2 1.9 collective-permute-start.4
  58.2 3.9 collective-permute-start.5
  62.1 0.1 fusion.335
  62.2 0.9 collective-permute-done.4
  63.1 6.2 %collective-permute-done.5 = f32[4,8,6,128]{3,2,1,0:T(8,128)S(1)} collective-permute-done((f32[4,8,6,128]{3,2,1,0:T(8,128)S(1)}, f32[4,8,6,128]{3,2,1,0:T(8,128)S(1)}, u32[]{:S(2)}, u32[]{:S(2)}) %collective-permute-start.5) | collective-permute-done | bytes 98336 | tf_op jit(solution)/shard_map/ppermute | solution.py:26
  69.3 1.6 fusion.134
  70.9 1.9 collective-permute-start.6
  72.9 3.9 collective-permute-start.7
  76.8 0.1 fusion.333
  76.9 0.9 collective-permute-done.6
  77.8 6.8 %collective-permute-done.7 = f32[4,8,6,128]{3,2,1,0:T(8,128)S(1)} collective-permute-done((f32[4,8,6,128]{3,2,1,0:T(8,128)S(1)}, f32[4,8,6,128]{3,2,1,0:T(8,128)S(1)}, u32[]{:S(2)}, u32[]{:S(2)}) %collective-permute-start.7) | collective-permute-done | bytes 98336 | tf_op jit(solution)/shard_map/ppermute | solution.py:26
  84.6 0.0 copy-done
  84.6 0.9 fusion.73
  85.5 1.9 collective-permute-start.8
  87.4 3.9 collective-permute-start.9
  91.3 0.1 fusion.331
  91.4 0.9 collective-permute-done.8
  92.3 6.1 %collective-permute-done.9 = f32[4,8,6,128]{3,2,1,0:T(8,128)S(1)} collective-permute-done((f32[4,8,6,128]{3,2,1,0:T(8,128)S(1)}, f32[4,8,6,128]{3,2,1,0:T(8,128)S(1)}, u32[]{:S(2)}, u32[]{:S(2)}) %collective-permute-start.9) | collective-permute-done | bytes 98336 | tf_op jit(solution)/shard_map/ppermute | solution.py:26
  98.5 0.9 fusion.12
  99.4 1.1 stack.11
  100.4 196.1 %all_to_all.5 = f32[32,2,4,8,8,128]{5,4,3,2,1,0:T(8,128)S(1)} all-to-all(f32[32,2,4,8,8,128]{5,4,3,2,1,0:T(8,128)S(1)} %stack.11), channel_id=1, replica_groups=mesh['band'=32,'dom'=16] {'band'}, dimensions={0} | all-to-all | bytes 16777216 | tf_op jit(solution)/shard_map/all_to_all | solution.py:79
  296.5 4.1 copy.7
  300.6 9.4 %reshape_reshape.3 = f32[256,8192]{1,0:T(8,128)} reshape(f32[2,32,4,8,8,128]{5,4,3,2,1,0:T(8,128)} %copy.7) | data formatting | bytes 16777216 | tf_op jit(solution)/shard_map/reshape;reshape | solution.py:81
  310.0 11.7 %fusion = f32[256,128]{1,0:T(8,128)S(1)} fusion(f32[256,8192]{1,0:T(8,128)} %reshape_reshape.3, f32[16,8,64,128]{3,2,1,0:T(8,128)} %bitcast.21), kind=kOutput, calls=%fused_computation | convolution fusion | flops 3221225472 | bytes 12713984 | tf_op jit(solution)/shard_map/dot_general | solution.py:82
  321.7 0.8 copy.8
  322.4 0.0 all-reduce.7.cloned.1.call-update
  322.5 161.3 %all-reduce.7.cloned.1.call-done = f32[128,2,128]{2,0,1:T(8,128)} async-done(((f32[128,2,128]{2,0,1:T(8,128)}), f32[128,2,128]{2,0,1:T(8,128)}) %all-reduce.7.cloned.1.call-update) | async-done | bytes 131088 | tf_op jit(solution)/shard_map/psum | solution.py:90
  483.8 1.5 slice_bitcast_fusion
  (6 shorter events, 0.1 us)
Async XLA Ops:
  7.2 77.4 %copy-start = (f32[8,8,128]{2,1,0:T(8,128)S(1)}, f32[8,8,128]{2,1,0:T(8,128)}, u32[]{:S(2)}) copy-start(f32[8,8,128]{2,1,0:T(8,128)} %param.5) | copy-start | bytes 98308
  7.2 476.6 %all-reduce.7.cloned.1.call-start = ((), (), s32[]{:S(2)}) async-start(), calls=%async_computation.1 | async-start | bytes 262144 | tf_op jit(solution)/shard_map/psum | solution.py:90
  8.2 18.7 %collective-permute-start = (f32[4,8,6,128]{3,2,1,0:T(8,128)S(1)}, f32[4,8,6,128]{3,2,1,0:T(8,128)S(1)}, u32[]{:S(2)}, u32[]{:S(2)}) collective-permute-start(f32[4,8,6,128]{3,2,1,0:T(8,128)S(1)} %get-tuple-element.22), channel_id=1, source_target_pairs={{1,0},{2,1},{3,2},{4,3},{5,4},{6,5},{7,6},{8,7},{9,8},{10,9},{11,1... | collective-permute-start | bytes 294920 | tf_op jit(solution)/shard_map/ppermute | solution.py:29
  21.4 13.1 %collective-permute-start.1 = (f32[4,8,6,128]{3,2,1,0:T(8,128)S(1)}, f32[4,8,6,128]{3,2,1,0:T(8,128)S(1)}, u32[]{:S(2)}, u32[]{:S(2)}) collective-permute-start(f32[4,8,6,128]{3,2,1,0:T(8,128)S(1)} %get-tuple-element.23), channel_id=1, source_target_pairs={{0,1},{1,2},{2,3},{3,4},{4,5},{5,6},{6,7},{7,8},{8,9},{9,10},{10,1... | collective-permute-start | bytes 294920 | tf_op jit(solution)/shard_map/ppermute | solution.py:26
  39.7 7.8 %collective-permute-start.2 = (f32[4,8,6,128]{3,2,1,0:T(8,128)S(1)}, f32[4,8,6,128]{3,2,1,0:T(8,128)S(1)}, u32[]{:S(2)}, u32[]{:S(2)}) collective-permute-start(f32[4,8,6,128]{3,2,1,0:T(8,128)S(1)} %get-tuple-element.18), channel_id=1, source_target_pairs={{1,0},{2,1},{3,2},{4,3},{5,4},{6,5},{7,6},{8,7},{9,8},{10,9},{11,1... | collective-permute-start | bytes 294920 | tf_op jit(solution)/shard_map/ppermute | solution.py:29
  41.6 12.8 %collective-permute-start.3 = (f32[4,8,6,128]{3,2,1,0:T(8,128)S(1)}, f32[4,8,6,128]{3,2,1,0:T(8,128)S(1)}, u32[]{:S(2)}, u32[]{:S(2)}) collective-permute-start(f32[4,8,6,128]{3,2,1,0:T(8,128)S(1)} %get-tuple-element.19), channel_id=1, source_target_pairs={{0,1},{1,2},{2,3},{3,4},{4,5},{5,6},{6,7},{7,8},{8,9},{9,10},{10,1... | collective-permute-start | bytes 294920 | tf_op jit(solution)/shard_map/ppermute | solution.py:26
  56.2 6.9 %collective-permute-start.4 = (f32[4,8,6,128]{3,2,1,0:T(8,128)S(1)}, f32[4,8,6,128]{3,2,1,0:T(8,128)S(1)}, u32[]{:S(2)}, u32[]{:S(2)}) collective-permute-start(f32[4,8,6,128]{3,2,1,0:T(8,128)S(1)} %get-tuple-element.14), channel_id=1, source_target_pairs={{1,0},{2,1},{3,2},{4,3},{5,4},{6,5},{7,6},{8,7},{9,8},{10,9},{11,1... | collective-permute-start | bytes 294920 | tf_op jit(solution)/shard_map/ppermute | solution.py:29
  58.2 11.1 %collective-permute-start.5 = (f32[4,8,6,128]{3,2,1,0:T(8,128)S(1)}, f32[4,8,6,128]{3,2,1,0:T(8,128)S(1)}, u32[]{:S(2)}, u32[]{:S(2)}) collective-permute-start(f32[4,8,6,128]{3,2,1,0:T(8,128)S(1)} %get-tuple-element.15), channel_id=1, source_target_pairs={{0,1},{1,2},{2,3},{3,4},{4,5},{5,6},{6,7},{7,8},{8,9},{9,10},{10,1... | collective-permute-start | bytes 294920 | tf_op jit(solution)/shard_map/ppermute | solution.py:26
  70.9 6.9 %collective-permute-start.6 = (f32[4,8,6,128]{3,2,1,0:T(8,128)S(1)}, f32[4,8,6,128]{3,2,1,0:T(8,128)S(1)}, u32[]{:S(2)}, u32[]{:S(2)}) collective-permute-start(f32[4,8,6,128]{3,2,1,0:T(8,128)S(1)} %get-tuple-element.10), channel_id=1, source_target_pairs={{1,0},{2,1},{3,2},{4,3},{5,4},{6,5},{7,6},{8,7},{9,8},{10,9},{11,1... | collective-permute-start | bytes 294920 | tf_op jit(solution)/shard_map/ppermute | solution.py:29
  72.9 11.7 %collective-permute-start.7 = (f32[4,8,6,128]{3,2,1,0:T(8,128)S(1)}, f32[4,8,6,128]{3,2,1,0:T(8,128)S(1)}, u32[]{:S(2)}, u32[]{:S(2)}) collective-permute-start(f32[4,8,6,128]{3,2,1,0:T(8,128)S(1)} %get-tuple-element.11), channel_id=1, source_target_pairs={{0,1},{1,2},{2,3},{3,4},{4,5},{5,6},{6,7},{7,8},{8,9},{9,10},{10,1... | collective-permute-start | bytes 294920 | tf_op jit(solution)/shard_map/ppermute | solution.py:26
  85.5 6.9 %collective-permute-start.8 = (f32[4,8,6,128]{3,2,1,0:T(8,128)S(1)}, f32[4,8,6,128]{3,2,1,0:T(8,128)S(1)}, u32[]{:S(2)}, u32[]{:S(2)}) collective-permute-start(f32[4,8,6,128]{3,2,1,0:T(8,128)S(1)} %get-tuple-element.6), channel_id=1, source_target_pairs={{1,0},{2,1},{3,2},{4,3},{5,4},{6,5},{7,6},{8,7},{9,8},{10,9},{11,1... | collective-permute-start | bytes 294920 | tf_op jit(solution)/shard_map/ppermute | solution.py:29
  87.4 11.1 %collective-permute-start.9 = (f32[4,8,6,128]{3,2,1,0:T(8,128)S(1)}, f32[4,8,6,128]{3,2,1,0:T(8,128)S(1)}, u32[]{:S(2)}, u32[]{:S(2)}) collective-permute-start(f32[4,8,6,128]{3,2,1,0:T(8,128)S(1)} %get-tuple-element.7), channel_id=1, source_target_pairs={{0,1},{1,2},{2,3},{3,4},{4,5},{5,6},{6,7},{7,8},{8,9},{9,10},{10,1... | collective-permute-start | bytes 294920 | tf_op jit(solution)/shard_map/ppermute | solution.py:26
Sparse Core Ops, SparseCore 0:
  322.6 161.1 all-reduce.6
